TPU v7x, 256 devices: a whole 4x4x8 slice. The times are simulated.
256 devices in a mesh: prow: 4 (over z_hi, core), pcol: 4 (over y), pl: 16 (over z_lo, x).
Axes of the slice: x: 4, y: 4, z: 8 (z_hi: 2, z_lo: 4; z = z_hi * 4 + z_lo), core: 2. Of those that a mesh axis runs over, the one named last changes fastest.
Arguments:
- factor_cols: bfloat16 [32768, 4096], P(('prow', 'pcol'), 'pl'), may hold values from -0.09375 to 0.09375
- modal_at_loads: bfloat16 [2048, 32768], P(None, ('prow', 'pcol')), may hold values from -0.03125 to 0.03125
- mode_shapes: bfloat16 [8192, 2048], P(('prow', 'pl')), may hold values from -0.125 to 0.125
- natural_freq: float32 [2048], replicated, may hold values from 0.5 to 2
- damping: float32 [2048], replicated, may hold values from 0.05 to 0.2
Outputs:
- cospectrum: float32 [8192, 8192], P(('prow', 'pl'), 'pcol')
All inputs are finite; a program needn't handle non-finite values.
Results may differ from a plain program's by a relative error of at most 0.022.
Values may be sent and summed in bfloat16 or wider, within the bound.
A program may use at most 128 MiB of HBM per device.

v0:
```python
import jax
import jax.numpy as jnp
from jax import lax
from jax.sharding import PartitionSpec as P


def transfer_pair(natural_freq, damping):
    detuning = natural_freq * natural_freq - 1.0
    damper = 2.0 * damping * natural_freq
    modulus = detuning * detuning + damper * damper
    return (detuning / modulus, -damper / modulus)


def outer_rows(left_rows, right_rows):
    return lax.dot_general(
        left_rows, right_rows, (((1,), (1,)), ((), ())), preferred_element_type=jnp.float32
    )


def make_body(n_row, n_col):
    swap = [(c * n_col + r, r * n_col + c) for r in range(n_row) for c in range(n_col)]

    def body(factor_cols, modal_at_loads, mode_shapes, natural_freq, damping):
        in_phase, quadrature = transfer_pair(natural_freq, damping)
        own_rows = lax.psum_scatter(
            jnp.dot(modal_at_loads, factor_cols, preferred_element_type=jnp.float32),
            ("prow", "pcol"),
            scatter_dimension=0,
            tiled=True,
        )
        modal_load = lax.all_gather(
            own_rows.astype(jnp.bfloat16), ("prow", "pcol"), axis=0, tiled=True
        )
        modal_wide = modal_load.astype(jnp.float32)
        pseudo = jnp.concatenate(
            [
                (in_phase[:, None] * modal_wide).astype(jnp.bfloat16),
                (quadrature[:, None] * modal_wide).astype(jnp.bfloat16),
            ],
            axis=1,
        )
        block = pseudo.shape[0] // (n_row * n_col)
        row, col = (lax.axis_index("prow"), lax.axis_index("pcol"))
        first_row = (col * n_row + row) * block
        own_pseudo = lax.dynamic_slice_in_dim(pseudo, first_row, block, 0)
        partial_gram = outer_rows(own_pseudo, pseudo)
        gram_block = lax.psum(partial_gram.astype(jnp.bfloat16), "pl")
        gram_panel = lax.all_gather(gram_block, "prow", axis=0, tiled=True)
        weighted_part = outer_rows(mode_shapes, gram_panel).astype(jnp.bfloat16)
        weighted = lax.all_gather(weighted_part, "pcol", axis=1, tiled=True)
        panel_piece = lax.ppermute(mode_shapes, ("prow", "pcol"), swap)
        return outer_rows(weighted, lax.all_gather(panel_piece, "pl", axis=0, tiled=True))

    return body


def solution(mesh):
    in_specs = (
        P(("prow", "pcol"), "pl"),
        P(None, ("prow", "pcol")),
        P(("prow", "pl"), None),
        P(),
        P(),
    )
    out_specs = P(("prow", "pl"), "pcol")
    body = make_body(mesh.shape["prow"], mesh.shape["pcol"])
    return jax.shard_map(body, mesh=mesh, in_specs=in_specs, out_specs=out_specs, check_vma=False)
```

profile of v0, /device:TPU:1, one launch (start us, length us, event | category | flops | bytes accessed | tf_op | source)
XLA Modules:
  0.0 488.3 jit_solution(12734103664353830712)
XLA Ops:
  6.5 1.2 copy-done
  7.8 7.1 %fusion.8 = f32[2048,256]{1,0:T(8,128)} fusion(bf16[2048,2048]{1,0:T(8,128)(2,1)} %param.6, bf16[2048,256]{1,0:T(8,128)(2,1)S(1)} %copy-done), kind=kOutput, calls=%fused_computation.18 | convolution fusion | flops 2147483648 | bytes 11534336 | tf_op jit(solution)/shard_map/dot_general | solution.py:26
  14.8 0.0 reduce-scatter.2.cloned.1.call-update
  14.9 0.0 all-gather.4.cloned.1.call-start
  14.9 90.0 %reduce-scatter.2.cloned.1.call-done = f32[128,256]{1,0:T(8,128)} async-done(((f32[2048,256]{1,0:T(8,128)}), f32[128,256]{1,0:T(8,128)}) %reduce-scatter.2.cloned.1.call-update) | async-done | bytes 131088 | tf_op jit(solution)/shard_map/reduce_scatter | solution.py:25
  104.9 1.5 convert_element_type.21
  106.5 0.0 all-gather.4.cloned.1.call-update
  106.5 0.0 all-reduce.2.cloned.1.call-start
  106.6 54.7 %all-gather.4.cloned.1.call-done = bf16[2048,256]{1,0:T(8,128)(2,1)} async-done(((bf16[128,256]{1,0:T(8,128)(2,1)}), bf16[2048,256]{1,0:T(8,128)(2,1)}) %all-gather.4.cloned.1.call-update) | async-done | bytes 1048592 | tf_op jit(solution)/shard_map/all_gather | solution.py:31
  161.3 1.8 fusion
  163.1 1.6 convolution_convert_fusion
  164.7 0.0 all-reduce.2.cloned.1.call-update
  164.7 0.0 all-gather.6.cloned.1.call-start
  164.7 146.3 %all-reduce.2.cloned.1.call-done = bf16[128,2048]{1,0:T(8,128)(2,1)} async-done(((bf16[128,2048]{1,0:T(8,128)(2,1)}), bf16[128,2048]{1,0:T(8,128)(2,1)}) %all-reduce.2.cloned.1.call-update) | async-done | bytes 524304 | tf_op jit(solution)/shard_map/psum | solution.py:47
  311.1 0.0 all-gather.6.cloned.1.call-update
  311.1 0.0 all-gather.8.cloned.1.call-start
  311.1 14.3 %collective-permute-start = (bf16[128,2048]{1,0:T(8,128)(2,1)S(1)}, bf16[128,2048]{1,0:T(8,128)(2,1)S(1)}, u32[]{:S(2)}, u32[]{:S(2)}) collective-permute-start(bf16[128,2048]{1,0:T(8,128)(2,1)S(1)} %copy-done.2), channel_id=1, source_target_pairs={{0,0},{64,16},{128,32},{192,48},{16,64},{80,80},{144,96},{208,112}... | collective-permute-start | bytes 1572872 | tf_op jit(solution)/shard_map/ppermute | solution.py:51
  325.4 7.8 %collective-permute-done = bf16[128,2048]{1,0:T(8,128)(2,1)S(1)} collective-permute-done((bf16[128,2048]{1,0:T(8,128)(2,1)S(1)}, bf16[128,2048]{1,0:T(8,128)(2,1)S(1)}, u32[]{:S(2)}, u32[]{:S(2)}) %collective-permute-start) | collective-permute-done | bytes 524320 | tf_op jit(solution)/shard_map/ppermute | solution.py:51
  333.2 0.8 copy-done.1
  334.1 34.2 %all-gather.6.cloned.1.call-done = bf16[512,2048]{1,0:T(8,128)(2,1)} async-done(((bf16[128,2048]{1,0:T(8,128)(2,1)}), bf16[512,2048]{1,0:T(8,128)(2,1)}) %all-gather.6.cloned.1.call-update) | async-done | bytes 2097168 | tf_op jit(solution)/shard_map/all_gather | solution.py:48
  368.3 2.3 fusion.2
  370.6 9.9 %all_gather.14 = bf16[128,2048]{0,1:T(8,128)(2,1)S(1)} all-gather(bf16[128,512]{0,1:T(8,128)(2,1)S(1)} %fusion.2), channel_id=1, replica_groups=mesh['prow'=4,'pcol'=4,'pl'=16] {'pcol'}, dimensions={1}, use_global_device_ids=true | all-gather | bytes 655360 | tf_op jit(solution)/shard_map/all_gather | solution.py:50
  380.5 94.0 %all-gather.8.cloned.1.call-done = bf16[2048,2048]{1,0:T(8,128)(2,1)} async-done(((bf16[128,2048]{1,0:T(8,128)(2,1)}), bf16[2048,2048]{1,0:T(8,128)(2,1)}) %all-gather.8.cloned.1.call-update) | async-done | bytes 8388624 | tf_op jit(solution)/shard_map/all_gather | solution.py:52
  474.5 7.3 %fusion.9 = f32[128,2048]{1,0:T(8,128)} fusion(bf16[128,2048]{0,1:T(8,128)(2,1)S(1)} %all_gather.14, bf16[2048,2048]{1,0:T(8,128)(2,1)} %all-gather.8.cloned.1.call-done), kind=kOutput, calls=%fused_computation.19 | convolution fusion | flops 1073741824 | bytes 9961472 | tf_op jit(solution)/shard_map/dot_general | solution.py:15
  (11 shorter events, 0.0 us)
Async XLA Ops:
  6.5 1.2 copy-start
  6.5 98.4 %reduce-scatter.2.cloned.1.call-start = ((), (), s32[]{:S(2)}) async-start(), calls=%async_computation.1 | async-start | bytes 2228224 | tf_op jit(solution)/shard_map/reduce_scatter | solution.py:25
  14.8 91.7 %copy-start.3 = (f32[2048]{0:T(1024)S(1)}, f32[2048]{0:T(1024)}, u32[]{:S(2)}) copy-start(f32[2048]{0:T(1024)} %param.8) | copy-start | bytes 24580
  14.8 91.7 %copy-start.4 = (f32[2048]{0:T(1024)S(1)}, f32[2048]{0:T(1024)}, u32[]{:S(2)}) copy-start(f32[2048]{0:T(1024)} %param.9) | copy-start | bytes 24580
  14.9 146.4 %all-gather.4.cloned.1.call-start = ((), (), s32[]{:S(2)}) async-start(), calls=%async_computation.2 | async-start | bytes 1114112 | tf_op jit(solution)/shard_map/all_gather | solution.py:31
  106.5 204.6 %all-reduce.2.cloned.1.call-start = ((), (), s32[]{:S(2)}) async-start(), calls=%async_computation.3 | async-start | bytes 1048576 | tf_op jit(solution)/shard_map/psum | solution.py:47
  163.0 148.1 %copy-start.2 = (bf16[128,2048]{1,0:T(8,128)(2,1)S(1)}, bf16[128,2048]{1,0:T(8,128)(2,1)}, u32[]{:S(2)}) copy-start(bf16[128,2048]{1,0:T(8,128)(2,1)} %param.7) | copy-start | bytes 1572868
  164.7 203.6 %all-gather.6.cloned.1.call-start = ((), (), s32[]{:S(2)}) async-start(), calls=%async_computation.4 | async-start | bytes 2621440 | tf_op jit(solution)/shard_map/all_gather | solution.py:48
  311.1 163.4 %all-gather.8.cloned.1.call-start = ((), (), s32[]{:S(2)}) async-start(), calls=%async_computation.5 | async-start | bytes 8912896 | tf_op jit(solution)/shard_map/all_gather | solution.py:52
  311.1 22.1 %collective-permute-start = (bf16[128,2048]{1,0:T(8,128)(2,1)S(1)}, bf16[128,2048]{1,0:T(8,128)(2,1)S(1)}, u32[]{:S(2)}, u32[]{:S(2)}) collective-permute-start(bf16[128,2048]{1,0:T(8,128)(2,1)S(1)} %copy-done.2), channel_id=1, source_target_pairs={{0,0},{64,16},{128,32},{192,48},{16,64},{80,80},{144,96},{208,112}... | collective-permute-start | bytes 1572872 | tf_op jit(solution)/shard_map/ppermute | solution.py:51
  333.2 0.8 copy-start.1
Sparse Core Ops, SparseCore 0:
  15.0 89.8 reduce-scatter.1
  107.7 53.5 all-gather.3
  164.8 146.2 all-reduce.1
  312.9 55.3 all-gather.5
  370.1 104.3 all-gather.7
where the time goes:
time: 489 us; the launch traced here: 488 us
  waiting for transfers between devices  427 us (87%)
  matrix products  18.3 us (4%)
  starting transfers between devices  14.5 us (3%)
  between operations  13.2 us (3%)
  blocking collectives  9.9 us (2%)
    psum x1, waiting for transfers between devices, body(): gram_block = lax.psum(partial_gram.astype(jnp.bfloat16), 'pl')  146 us
    all_gather x1, waiting for transfers between devices, body(): lax.all_gather(panel_piece, 'pl', axis=0, tiled=True)  94 us
    reduce_scatter x1, waiting for transfers between devices, body(): lax.psum_scatter(jnp.dot(modal_at_loads, factor_cols, preferred_element_t...  90 us
    all_gather x1, waiting for transfers between devices, body(): lax.all_gather(own_rows.astype(jnp.bfloat16), ('prow', 'pcol'), axis=0, t...  54.7 us
    all_gather x1, waiting for transfers between devices, body(): gram_panel = lax.all_gather(gram_block, 'prow', axis=0, tiled=True)  34.2 us
    ppermute x1, starting transfers between devices, body(): panel_piece = lax.ppermute(mode_shapes, ('prow', 'pcol'), swap)  14.3 us
    dot_general x3, matrix products, outer_rows(): lax.dot_general(left_rows, right_rows, (((1,), (1,)), ((), ())), preferre...  11.2 us
    all_gather x1, blocking collectives, body(): weighted = lax.all_gather(weighted_part, 'pcol', axis=1, tiled=True)  9.9 us
  transfers between devices with their start and end apart: 6, of which 6 were waited for; matrix products, arithmetic and copies ran while one was open for 0% of the time, Pallas kernels for 0%

commit v1 on v0

--- a/solution.py
+++ b/solution.py
@@ -2,6 +2,12 @@
 import jax.numpy as jnp
 from jax import lax
 from jax.sharding import PartitionSpec as P
+
+
+def add_all(shard, axis):
+    shards = lax.all_gather(shard, axis, axis=0, tiled=False)
+    summed = shards.sum(axis=0)
+    return summed
 
 
 def transfer_pair(natural_freq, damping):
@@ -44,7 +50,7 @@
         first_row = (col * n_row + row) * block
         own_pseudo = lax.dynamic_slice_in_dim(pseudo, first_row, block, 0)
         partial_gram = outer_rows(own_pseudo, pseudo)
-        gram_block = lax.psum(partial_gram.astype(jnp.bfloat16), "pl")
+        gram_block = add_all(partial_gram.astype(jnp.bfloat16), "pl")
         gram_panel = lax.all_gather(gram_block, "prow", axis=0, tiled=True)
         weighted_part = outer_rows(mode_shapes, gram_panel).astype(jnp.bfloat16)
         weighted = lax.all_gather(weighted_part, "pcol", axis=1, tiled=True)

time: 489 us -> 438 us (0.90)
  waiting for transfers between devices: 427 us -> 381 us
  starting transfers between devices: 14.5 us -> 3.84 us
  other arithmetic: 3.3 us -> 9.49 us
    psum x1 -> x0, waiting for transfers between devices: 146 us -> none  [body(): gram_block = lax.psum(partial_gram.astype(jnp.bfloat16), 'pl')]
    all_gather x0 -> x1, waiting for transfers between devices: none -> 97.7 us  [add_all(): shards = lax.all_gather(shard, axis, axis=0, tiled=False)]
    ppermute x1, starting transfers between devices: 14.3 us -> 3.67 us  [body(): panel_piece = lax.ppermute(mode_shapes, ('prow', 'pcol'), swap)]
    reduce_sum x0 -> x1, other arithmetic: none -> 6.19 us  [add_all(): summed = shards.sum(axis=0)]
  transfers between devices with their start and end apart: 6 -> 6, of which waited for: 6 -> 6; matrix products, arithmetic and copies ran while one was open for 0% -> 1% of each run, Pallas kernels for 0% -> 0%
where the time goes in v1:
time: 438 us
  waiting for transfers between devices  381 us (87%)
  matrix products  18.3 us (4%)
  between operations  13.2 us (3%)
  blocking collectives  9.9 us (2%)
  other arithmetic  9.49 us (2%)
    all_gather x1, waiting for transfers between devices, add_all(): shards = lax.all_gather(shard, axis, axis=0, tiled=False)  97.7 us
    all_gather x1, waiting for transfers between devices, body(): lax.all_gather(panel_piece, 'pl', axis=0, tiled=True)  96.3 us
    reduce_scatter x1, waiting for transfers between devices, body(): lax.psum_scatter(jnp.dot(modal_at_loads, factor_cols, preferred_element_t...  90 us
    all_gather x1, waiting for transfers between devices, body(): lax.all_gather(own_rows.astype(jnp.bfloat16), ('prow', 'pcol'), axis=0, t...  54.7 us
    all_gather x1, waiting for transfers between devices, body(): gram_panel = lax.all_gather(gram_block, 'prow', axis=0, tiled=True)  35.4 us
    dot_general x3, matrix products, outer_rows(): lax.dot_general(left_rows, right_rows, (((1,), (1,)), ((), ())), preferre...  11.2 us
    all_gather x1, blocking collectives, body(): weighted = lax.all_gather(weighted_part, 'pcol', axis=1, tiled=True)  9.9 us
  transfers between devices with their start and end apart: 6, of which 6 were waited for; matrix products, arithmetic and copies ran while one was open for 1% of the time, Pallas kernels for 0%

profile of v1, /device:TPU:1, one launch (start us, length us, event | category | flops | bytes accessed | tf_op | source)
XLA Modules:
  0.0 437.8 jit_solution(12797681611252640683)
XLA Ops:
  6.5 1.2 copy-done
  7.8 7.1 %fusion.8 = f32[2048,256]{1,0:T(8,128)} fusion(bf16[2048,2048]{1,0:T(8,128)(2,1)} %param.6, bf16[2048,256]{1,0:T(8,128)(2,1)S(1)} %copy-done), kind=kOutput, calls=%fused_computation.18 | convolution fusion | flops 2147483648 | bytes 11534336 | tf_op jit(solution)/shard_map/dot_general | solution.py:32
  14.8 0.0 reduce-scatter.2.cloned.1.call-update
  14.9 0.0 all-gather.6.cloned.1.call-start
  14.9 90.0 %reduce-scatter.2.cloned.1.call-done = f32[128,256]{1,0:T(8,128)} async-done(((f32[2048,256]{1,0:T(8,128)}), f32[128,256]{1,0:T(8,128)}) %reduce-scatter.2.cloned.1.call-update) | async-done | bytes 131088 | tf_op jit(solution)/shard_map/reduce_scatter | solution.py:31
  104.9 1.5 convert_element_type.23
  106.5 0.0 all-gather.6.cloned.1.call-update
  106.5 0.0 all-gather.12.cloned.1.call-start
  106.6 54.7 %all-gather.6.cloned.1.call-done = bf16[2048,256]{1,0:T(8,128)(2,1)} async-done(((bf16[128,256]{1,0:T(8,128)(2,1)}), bf16[2048,256]{1,0:T(8,128)(2,1)}) %all-gather.6.cloned.1.call-update) | async-done | bytes 1048592 | tf_op jit(solution)/shard_map/all_gather | solution.py:37
  161.3 1.8 fusion
  163.0 1.6 convolution_convert_fusion
  164.6 0.0 all-gather.12.cloned.1.call-update
  164.7 0.0 all-gather.8.cloned.1.call-start
  164.7 97.7 %all-gather.12.cloned.1.call-done = bf16[2048,2048]{1,0:T(8,128)(2,1)} async-done(((bf16[128,2048]{1,0:T(8,128)(2,1)}), bf16[2048,2048]{1,0:T(8,128)(2,1)}) %all-gather.12.cloned.1.call-update) | async-done | bytes 8388624 | tf_op jit(solution)/shard_map/all_gather | solution.py:8
  262.5 6.2 %reduce_sum.12 = bf16[128,2048]{1,0:T(8,128)(2,1)} reduce(bf16[16,128,2048]{2,1,0:T(8,128)(2,1)} %bitcast.9, bf16[]{:T(256)} %constant.25.clone.1), dimensions={0}, to_apply=%region_1.0 | reduce | flops 3932160 | bytes 8912898 | tf_op jit(solution)/shard_map/reduce_sum | solution.py:9
  268.7 0.0 all-gather.10.cloned.1.call-start
  268.7 3.7 collective-permute-start
  272.4 6.8 %collective-permute-done = bf16[128,2048]{1,0:T(8,128)(2,1)S(1)} collective-permute-done((bf16[128,2048]{1,0:T(8,128)(2,1)S(1)}, bf16[128,2048]{1,0:T(8,128)(2,1)S(1)}, u32[]{:S(2)}, u32[]{:S(2)}) %collective-permute-start) | collective-permute-done | bytes 524320 | tf_op jit(solution)/shard_map/ppermute | solution.py:57
  279.3 0.8 copy-done.1
  280.1 35.4 %all-gather.8.cloned.1.call-done = bf16[512,2048]{1,0:T(8,128)(2,1)} async-done(((bf16[128,2048]{1,0:T(8,128)(2,1)}), bf16[512,2048]{1,0:T(8,128)(2,1)}) %all-gather.8.cloned.1.call-update) | async-done | bytes 2097168 | tf_op jit(solution)/shard_map/all_gather | solution.py:54
  315.5 2.3 fusion.2
  317.8 9.9 %all_gather.22 = bf16[128,2048]{0,1:T(8,128)(2,1)S(1)} all-gather(bf16[128,512]{0,1:T(8,128)(2,1)S(1)} %fusion.2), channel_id=1, replica_groups=mesh['prow'=4,'pcol'=4,'pl'=16] {'pcol'}, dimensions={1}, use_global_device_ids=true | all-gather | bytes 655360 | tf_op jit(solution)/shard_map/all_gather | solution.py:56
  327.7 96.3 %all-gather.10.cloned.1.call-done = bf16[2048,2048]{1,0:T(8,128)(2,1)} async-done(((bf16[128,2048]{1,0:T(8,128)(2,1)}), bf16[2048,2048]{1,0:T(8,128)(2,1)}) %all-gather.10.cloned.1.call-update) | async-done | bytes 8388624 | tf_op jit(solution)/shard_map/all_gather | solution.py:58
  424.0 7.3 %fusion.9 = f32[128,2048]{1,0:T(8,128)} fusion(bf16[128,2048]{0,1:T(8,128)(2,1)S(1)} %all_gather.22, bf16[2048,2048]{1,0:T(8,128)(2,1)} %all-gather.10.cloned.1.call-done), kind=kOutput, calls=%fused_computation.19 | convolution fusion | flops 1073741824 | bytes 9961472 | tf_op jit(solution)/shard_map/dot_general | solution.py:21
  (12 shorter events, 0.1 us)
Async XLA Ops:
  6.5 1.2 copy-start
  6.5 98.4 %reduce-scatter.2.cloned.1.call-start = ((), (), s32[]{:S(2)}) async-start(), calls=%async_computation.1 | async-start | bytes 2228224 | tf_op jit(solution)/shard_map/reduce_scatter | solution.py:31
  14.8 91.7 %copy-start.3 = (f32[2048]{0:T(1024)S(1)}, f32[2048]{0:T(1024)}, u32[]{:S(2)}) copy-start(f32[2048]{0:T(1024)} %param.8) | copy-start | bytes 24580
  14.8 91.7 %copy-start.4 = (f32[2048]{0:T(1024)S(1)}, f32[2048]{0:T(1024)}, u32[]{:S(2)}) copy-start(f32[2048]{0:T(1024)} %param.9) | copy-start | bytes 24580
  14.9 146.4 %all-gather.6.cloned.1.call-start = ((), (), s32[]{:S(2)}) async-start(), calls=%async_computation.2 | async-start | bytes 1114112 | tf_op jit(solution)/shard_map/all_gather | solution.py:37
  106.5 156.0 %all-gather.12.cloned.1.call-start = ((), (), s32[]{:S(2)}) async-start(), calls=%async_computation.5 | async-start | bytes 8912896 | tf_op jit(solution)/shard_map/all_gather | solution.py:8
  164.7 150.8 %all-gather.8.cloned.1.call-start = ((), (), s32[]{:S(2)}) async-start(), calls=%async_computation.3 | async-start | bytes 2621440 | tf_op jit(solution)/shard_map/all_gather | solution.py:54
  262.5 6.3 %copy-start.2 = (bf16[128,2048]{1,0:T(8,128)(2,1)S(1)}, bf16[128,2048]{1,0:T(8,128)(2,1)}, u32[]{:S(2)}) copy-start(bf16[128,2048]{1,0:T(8,128)(2,1)} %param.7) | copy-start | bytes 1572868
  268.7 155.4 %all-gather.10.cloned.1.call-start = ((), (), s32[]{:S(2)}) async-start(), calls=%async_computation.4 | async-start | bytes 8912896 | tf_op jit(solution)/shard_map/all_gather | solution.py:58
  268.7 10.5 %collective-permute-start = (bf16[128,2048]{1,0:T(8,128)(2,1)S(1)}, bf16[128,2048]{1,0:T(8,128)(2,1)S(1)}, u32[]{:S(2)}, u32[]{:S(2)}) collective-permute-start(bf16[128,2048]{1,0:T(8,128)(2,1)S(1)} %copy-done.2), channel_id=1, source_target_pairs={{0,0},{64,16},{128,32},{192,48},{16,64},{80,80},{144,96},{208,112}... | collective-permute-start | bytes 1572872 | tf_op jit(solution)/shard_map/ppermute | solution.py:57
  279.3 0.8 copy-start.1
Sparse Core Ops, SparseCore 0:
  15.0 89.8 reduce-scatter.1
  107.7 53.5 all-gather.5
  164.8 97.6 all-gather.11
  268.8 46.6 all-gather.7
  317.1 106.8 all-gather.9
